TPU v7x, 128 devices: a whole 4x4x4 slice. The times are simulated.
128 devices in a mesh: ctx: 8 (over y, x_lo), tp: 16 (over x_hi, z, core).
Axes of the slice: x: 4 (x_hi: 2, x_lo: 2; x = x_hi * 2 + x_lo), y: 4, z: 4, core: 2. Of those that a mesh axis runs over, the one named last changes fastest.
Arguments:
- tokens: bfloat16 [4096, 4096], P(('ctx', 'tp')), may hold values from -16 to 16
- upstream: bfloat16 [4096, 4096], P('ctx', 'tp'), may hold values from -6 to 6
- w_query: bfloat16 [4096, 4096], P('ctx', 'tp')
- w_keyval: bfloat16 [4096, 2048], P('ctx', 'tp')
- positions: int32 [4096], replicated, may hold values from 0 to 4095, as said below
- documents: int32 [4096], replicated, may hold values from 0 to 3, never falling along the last dimension, each value on 1 to 2048 neighbouring positions
Outputs:
- token_grad: bfloat16 [4096, 4096], P(('ctx', 'tp'))
- query_grad: float32 [4096, 4096], P('ctx', 'tp')
- keyval_grad: float32 [4096, 2048], P('ctx', 'tp')
Inputs may be any that keep to these rules, and one draw needn't show every extreme that they name: Each stored run of 512 tokens holds consecutive increasing positions; the two runs of the tokens of one context rank are the blocks k and 15 - k of the sequence for some k; all runs together hold every position once.
All inputs are finite; a program needn't handle non-finite values.
Results may differ from a plain program's by a relative error of at most 0.02.
The roundings to bfloat16 on the way count: a program that leaves them out, or rounds other values in their place, can miss the bound.
Values may be sent and summed in bfloat16 or wider, within the bound.
A program may use at most 128 MiB of HBM per device.

v0:
```python
import jax
import jax.numpy as jnp
from jax import lax
from jax.sharding import PartitionSpec as P

KEY_VALUE_HEADS = 8
HEAD_DIMENSION = 128
rope_base = 500000.0


def side_by_side(arrays, axis, dim, along):
    both = jnp.concatenate(arrays, axis=along)
    filled, at, gathered = (lax.all_gather(both, axis, axis=dim, tiled=True), 0, [])
    for a in arrays:
        gathered.append(lax.slice_in_dim(filled, at, at + a.shape[along], axis=along))
        at += a.shape[along]
    return tuple(gathered)


def partner_2(block, axis, bit):
    count = lax.axis_size(axis)
    route = []
    for low in range(count):
        high = low | 1 << bit
        if high != low and high < count:
            route += [(low, high), (high, low)]
    return lax.ppermute(block, axis, route)


def copy_for_each(x, axis):
    count = lax.axis_size(axis)
    return lax.all_to_all(jnp.broadcast_to(x[None], (count, *x.shape)), axis, 0, 0, tiled=True)


def laid_out(blocks, dim):
    lengths = list(blocks.shape[1:])
    lengths[dim] *= blocks.shape[0]
    return jnp.moveaxis(blocks, 0, dim).reshape(lengths)


def gathered_copies(x, axis, dim):
    blocks = copy_for_each(x, axis)
    return laid_out(blocks, dim)


def cut_along(x, dim, count):
    lengths = x.shape
    blocks = x.reshape(*lengths[:dim], count, lengths[dim] // count, *lengths[dim + 1 :])
    return jnp.moveaxis(blocks, dim, 0)


def summed_on_arrival(x, axis, dim):
    count = lax.axis_size(axis)
    blocks = lax.all_to_all(cut_along(x, dim, count), axis, 0, 0, tiled=True)
    return jnp.sum(blocks.astype(jnp.float32), axis=0)


def rotation_tables(positions):
    half_width = HEAD_DIMENSION // 2
    frequency = rope_base ** (-(jnp.arange(half_width, dtype=jnp.float32) * 2.0 / HEAD_DIMENSION))
    angles = positions.astype(jnp.float32)[:, None] * frequency[None, :]
    cosine = jnp.concatenate([jnp.cos(angles), jnp.cos(angles)], axis=1)
    sine = jnp.concatenate([jnp.sin(angles), jnp.sin(angles)], axis=1)
    return (cosine, sine)


def rotate(values, cosine, sine):
    half_width = values.shape[-1] // 2
    turned = jnp.concatenate([-values[..., half_width:], values[..., :half_width]], axis=-1)
    return values * cosine[:, None, :] + turned * sine[:, None, :]


def rotate_back(gradient, cosine, sine):
    half_width = gradient.shape[-1] // 2
    scaled = gradient * sine[:, None, :]
    turned = jnp.concatenate([scaled[..., half_width:], -scaled[..., :half_width]], axis=-1)
    return gradient * cosine[:, None, :] + turned


def attend(
    query_rows, grad_out, keys_all, values_all, query_pos, query_doc, key_pos, key_doc, scaling
):
    f32 = jnp.float32
    tok_rows, head_count, head_width = query_rows.shape
    block_rows = min(tok_rows, 128)
    block_count = tok_rows // block_rows
    seq_len = keys_all.shape[0]

    def advance(totals, inputs):
        key_total, value_total = totals
        query_block, grad_block, pos_block, doc_block = inputs
        scores = (
            jnp.einsum("qhd,kd->hqk", query_block, keys_all, preferred_element_type=f32) * scaling
        )
        visible = (key_pos[None, :] <= pos_block[:, None]) & (
            key_doc[None, :] == doc_block[:, None]
        )
        scores = jnp.where(visible[None], scores, -1e30)
        row_peak = jnp.max(scores, axis=-1, keepdims=True)
        exponent = jnp.exp(scores - row_peak)
        probs = exponent / jnp.sum(exponent, axis=-1, keepdims=True)
        probs_half = probs.astype(jnp.bfloat16)
        output = jnp.einsum("hqk,kd->qhd", probs_half, values_all, preferred_element_type=f32)
        deltas = jnp.sum(grad_block.astype(f32) * output, axis=-1)
        prob_grad = jnp.einsum("qhd,kd->hqk", grad_block, values_all, preferred_element_type=f32)
        score_grad = (probs * (prob_grad - deltas.T[:, :, None])).astype(jnp.bfloat16)
        dquery = (
            jnp.einsum("hqk,kd->qhd", score_grad, keys_all, preferred_element_type=f32) * scaling
        )
        key_total = (
            key_total
            + jnp.einsum("hqk,qhd->kd", score_grad, query_block, preferred_element_type=f32)
            * scaling
        )
        value_total = value_total + jnp.einsum(
            "hqk,qhd->kd", probs_half, grad_block, preferred_element_type=f32
        )
        return ((key_total, value_total), dquery)

    blank_keys = jnp.zeros((seq_len, head_width), f32)
    inputs = (
        query_rows.reshape(block_count, block_rows, head_count, head_width),
        grad_out.reshape(block_count, block_rows, head_count, head_width),
        query_pos.reshape(block_count, block_rows),
        query_doc.reshape(block_count, block_rows),
    )
    (key_total, value_total), dquery = lax.scan(advance, (blank_keys, blank_keys), inputs)
    return (dquery.reshape(tok_rows, head_count, head_width), key_total, value_total)


def shards(tokens, upstream, w_query, w_keyval, positions, documents):
    f32 = jnp.float32
    ctx_rank = lax.axis_index("ctx")
    tp_rank = lax.axis_index("tp")
    tensor_split_count = lax.axis_size("tp")
    gathered = lax.all_gather(tokens, "tp", axis=0, tiled=True)
    tok_rows = gathered.shape[0]
    query_cols = w_query.shape[1]
    head_count = query_cols // HEAD_DIMENSION
    pairing_flags = (tensor_split_count // KEY_VALUE_HEADS).bit_length() - 1
    doc_all = jnp.take(documents, positions)
    cosine_all, sine_all = rotation_tables(positions)
    row_offset = ctx_rank * tok_rows
    my_pos = lax.dynamic_slice_in_dim(positions, row_offset, tok_rows, 0)
    my_doc = lax.dynamic_slice_in_dim(doc_all, row_offset, tok_rows, 0)
    my_cos = lax.dynamic_slice_in_dim(cosine_all, row_offset, tok_rows, 0)
    my_sin = lax.dynamic_slice_in_dim(sine_all, row_offset, tok_rows, 0)
    query_full, keyval_full = side_by_side((w_query, w_keyval), "ctx", 0, 1)
    query_raw = jnp.dot(gathered, query_full, preferred_element_type=f32)
    keyval_raw = jnp.dot(gathered, keyval_full, preferred_element_type=f32)
    query_rot = rotate(
        query_raw.reshape(tok_rows, head_count, HEAD_DIMENSION), my_cos, my_sin
    ).astype(jnp.bfloat16)
    head_kv = keyval_raw.astype(jnp.bfloat16)
    bit_index = 0
    partner = partner_2(head_kv, "tp", bit_index)
    is_lower = tp_rank // (1 << bit_index) % 2 == 0
    head_kv = jnp.where(
        is_lower,
        jnp.concatenate([head_kv, partner], axis=1),
        jnp.concatenate([partner, head_kv], axis=1),
    )
    key_rot = rotate(head_kv[:, None, :HEAD_DIMENSION].astype(f32), my_cos, my_sin)[:, 0].astype(
        jnp.bfloat16
    )
    local_kv = jnp.concatenate([key_rot, head_kv[:, HEAD_DIMENSION:]], axis=1)
    key_value = gathered_copies(local_kv, "ctx", 0)
    grad_query, grad_key, grad_value = attend(
        query_rot,
        upstream.reshape(tok_rows, head_count, HEAD_DIMENSION),
        key_value[:, :HEAD_DIMENSION],
        key_value[:, HEAD_DIMENSION:],
        my_pos,
        my_doc,
        positions,
        doc_all,
        HEAD_DIMENSION ** (-0.5),
    )
    query_back = (
        rotate_back(grad_query, my_cos, my_sin).astype(jnp.bfloat16).reshape(tok_rows, query_cols)
    )
    key_backward = rotate_back(grad_key[:, None, :], cosine_all, sine_all)[:, 0]
    key_terms = jnp.concatenate([key_backward, grad_value], axis=1)
    head_grad = summed_on_arrival(key_terms.astype(jnp.bfloat16), "ctx", 0)
    for bit_index in reversed(range(pairing_flags)):
        half_width = head_grad.shape[1] // 2
        lower_half = head_grad[:, :half_width]
        upper_half = head_grad[:, half_width:]
        is_lower = tp_rank // (1 << bit_index) % 2 == 0
        retained = jnp.where(is_lower, lower_half, upper_half)
        outgoing = jnp.where(is_lower, upper_half, lower_half)
        head_grad = retained + partner_2(outgoing.astype(jnp.bfloat16), "tp", bit_index).astype(
            outgoing.dtype
        )
    key_value_backward = head_grad.astype(jnp.bfloat16)
    row_grads = jnp.concatenate([query_back, key_value_backward], axis=1)
    part_query = lax.dot_general(
        row_grads[:, :query_cols], query_full, (((1,), (1,)), ((), ())), preferred_element_type=f32
    )
    part_keyval = lax.dot_general(
        row_grads[:, query_cols:], keyval_full, (((1,), (1,)), ((), ())), preferred_element_type=f32
    )
    token_grad = lax.psum_scatter(
        (part_query + part_keyval).astype(jnp.bfloat16), "tp", scatter_dimension=0, tiled=True
    )
    weight_grad = summed_on_arrival(
        lax.dot_general(
            gathered, row_grads, (((0,), (0,)), ((), ())), preferred_element_type=f32
        ).astype(jnp.bfloat16),
        "ctx",
        0,
    )
    return (token_grad, weight_grad[:, :query_cols], weight_grad[:, query_cols:])


def solution(mesh):
    return jax.shard_map(
        shards,
        mesh=mesh,
        in_specs=(P(("ctx", "tp"), None), P("ctx", "tp"), P("ctx", "tp"), P("ctx", "tp"), P(), P()),
        out_specs=(P(("ctx", "tp"), None), P("ctx", "tp"), P("ctx", "tp")),
        check_vma=False,
    )
```

profile of v0, /device:TPU:0, one launch (start us, length us, event | category | flops | bytes accessed | tf_op | source)
XLA Modules:
  0.0 420.5 jit_solution(1429676096698661029)
XLA Ops:
  10.5 23.0 %gather_fusion = s32[4096]{0:T(1024)S(1)} fusion(s32[4096]{0:T(1024)S(1)} %copy-done, s32[4096]{0:T(1024)S(1)} %fusion.68), kind=kCustom, calls=%fused_computation | custom fusion | bytes 49152 | tf_op jit(solution)/shard_map/jit(_take)/gather | solution.py:141
  33.6 50.6 %all-gather.3.cloned.1.call-done = bf16[4096,384]{1,0:T(8,128)(2,1)} async-done(((bf16[512,384]{1,0:T(8,128)(2,1)}), bf16[4096,384]{1,0:T(8,128)(2,1)}) %all-gather.3.cloned.1.call-update) | async-done | bytes 3145744 | tf_op jit(solution)/shard_map/all_gather | solution.py:13
  84.2 57.0 %all-gather.5.cloned.1.call-done = bf16[512,4096]{1,0:T(8,128)(2,1)} async-done(((bf16[32,4096]{1,0:T(8,128)(2,1)}), bf16[512,4096]{1,0:T(8,128)(2,1)}) %all-gather.5.cloned.1.call-update) | async-done | bytes 4194320 | tf_op jit(solution)/shard_map/all_gather | solution.py:136
  141.2 4.0 fusion.52
  145.5 3.7 multiply_cosine_fusion
  152.2 4.4 %all-to-all-start = ((bf16[8,512,256]{1,2,0:T(8,128)(2,1)}), bf16[8,512,256]{1,2,0:T(8,128)(2,1)S(1)}, u32[]{:S(2)}, u32[]{:S(2)}) async-start(bf16[8,512,256]{1,2,0:T(8,128)(2,1)} %broadcast_in_dim.33), calls=%async_computation | async-start | bytes 4194304 | tf_op jit(solution)/shard_map/all_to_all | solution.py:32
  157.5 4.1 fusion.50
  171.2 12.9 %all-to-all-done = bf16[8,512,256]{1,2,0:T(8,128)(2,1)S(1)} async-done(((bf16[8,512,256]{1,2,0:T(8,128)(2,1)}), bf16[8,512,256]{1,2,0:T(8,128)(2,1)S(1)}, u32[]{:S(2)}, u32[]{:S(2)}) %all-to-all-start) | async-done | bytes 2097184 | tf_op jit(solution)/shard_map/all_to_all | solution.py:32
  189.6 89.4 %while.15 = (s32[]{:T(128)}, f32[4096,128]{1,0:T(8,128)}, f32[4096,128]{1,0:T(8,128)}, f32[4,128,2,128]{3,1,2,0:T(8,128)}, s32[4096]{0:T(1024)S(1)}, /*index=5*/...) while((s32[]{:T(128)}, f32[4096,128]{1,0:T(8,128)}, ...), condition=%wide.region_4.5_spmd.clone, body=%wide.region_0.4_spmd.clone.sunk | while | flops 1625427712 | bytes 64595660 | solution.py:127
  190.1 4.9 %fusion.118 = (f32[2,128]{1,0:T(2,128)S(1)}, f32[2,128,4096]{2,1,0:T(8,128)}) fusion(pred[128,4096]{1,0:T(8,128)(4,1)S(1)} %compare_and_fusion.2, bf16[4096,128]{1,0:T(8,128)(2,1)} %get-tuple-element.330, bf16[4,128,2,128]{3,1,2,0:T(8,128)(2,1)} %get-tuple-element.329, s32[]{:T(128)} %get-tuple-element.307), kind=kOutput, calls=%fused_computation.112.clone.1 | convolution fusion | flops 272633856 | bytes 5834240 | tf_op jit(solution)/shard_map/while/body/eval_jaxpr/sub | solution.py:100
  201.6 4.0 fusion.122
  210.8 4.9 %fusion.118 = (f32[2,128]{1,0:T(2,128)S(1)}, f32[2,128,4096]{2,1,0:T(8,128)}) fusion(pred[128,4096]{1,0:T(8,128)(4,1)S(1)} %compare_and_fusion.2, bf16[4096,128]{1,0:T(8,128)(2,1)} %get-tuple-element.330, bf16[4,128,2,128]{3,1,2,0:T(8,128)(2,1)} %get-tuple-element.329, s32[]{:T(128)} %get-tuple-element.307), kind=kOutput, calls=%fused_computation.112.clone.1 | convolution fusion | flops 272633856 | bytes 5834240 | tf_op jit(solution)/shard_map/while/body/eval_jaxpr/sub | solution.py:100
  222.3 4.6 %fusion.122 = f32[4096,128]{1,0:T(8,128)} fusion(bf16[2,128,4096]{2,1,0:T(8,128)(2,1)} %fusion.121, f32[4096,128]{1,0:T(8,128)} %get-tuple-element.308, pred[]{:T(512)S(6)} %compare.5, bf16[4,128,2,128]{3,1,2,0:T(8,128)(2,1)} %get-tuple-element.329, s32[]{:T(128)} %get-tuple-element.307), kind=kOutput, calls=%fused_computation.14.clone.1 | convolution fusion | flops 270008320 | bytes 6357505 | tf_op jit(solution)/shard_map/while/body/eval_jaxpr/hqk,qhd->kd/dot_general | solution.py:112
  233.7 4.9 %fusion.118 = (f32[2,128]{1,0:T(2,128)S(1)}, f32[2,128,4096]{2,1,0:T(8,128)}) fusion(pred[128,4096]{1,0:T(8,128)(4,1)S(1)} %compare_and_fusion.2, bf16[4096,128]{1,0:T(8,128)(2,1)} %get-tuple-element.330, bf16[4,128,2,128]{3,1,2,0:T(8,128)(2,1)} %get-tuple-element.329, s32[]{:T(128)} %get-tuple-element.307), kind=kOutput, calls=%fused_computation.112.clone.1 | convolution fusion | flops 272633856 | bytes 5834240 | tf_op jit(solution)/shard_map/while/body/eval_jaxpr/sub | solution.py:100
  245.2 4.6 %fusion.122 = f32[4096,128]{1,0:T(8,128)} fusion(bf16[2,128,4096]{2,1,0:T(8,128)(2,1)} %fusion.121, f32[4096,128]{1,0:T(8,128)} %get-tuple-element.308, pred[]{:T(512)S(6)} %compare.5, bf16[4,128,2,128]{3,1,2,0:T(8,128)(2,1)} %get-tuple-element.329, s32[]{:T(128)} %get-tuple-element.307), kind=kOutput, calls=%fused_computation.14.clone.1 | convolution fusion | flops 270008320 | bytes 6357505 | tf_op jit(solution)/shard_map/while/body/eval_jaxpr/hqk,qhd->kd/dot_general | solution.py:112
  252.4 3.7 fusion.123
  256.6 4.9 %fusion.118 = (f32[2,128]{1,0:T(2,128)S(1)}, f32[2,128,4096]{2,1,0:T(8,128)}) fusion(pred[128,4096]{1,0:T(8,128)(4,1)S(1)} %compare_and_fusion.2, bf16[4096,128]{1,0:T(8,128)(2,1)} %get-tuple-element.330, bf16[4,128,2,128]{3,1,2,0:T(8,128)(2,1)} %get-tuple-element.329, s32[]{:T(128)} %get-tuple-element.307), kind=kOutput, calls=%fused_computation.112.clone.1 | convolution fusion | flops 272633856 | bytes 5834240 | tf_op jit(solution)/shard_map/while/body/eval_jaxpr/sub | solution.py:100
  268.1 4.6 %fusion.122 = f32[4096,128]{1,0:T(8,128)} fusion(bf16[2,128,4096]{2,1,0:T(8,128)(2,1)} %fusion.121, f32[4096,128]{1,0:T(8,128)} %get-tuple-element.308, pred[]{:T(512)S(6)} %compare.5, bf16[4,128,2,128]{3,1,2,0:T(8,128)(2,1)} %get-tuple-element.329, s32[]{:T(128)} %get-tuple-element.307), kind=kOutput, calls=%fused_computation.14.clone.1 | convolution fusion | flops 270008320 | bytes 6357505 | tf_op jit(solution)/shard_map/while/body/eval_jaxpr/hqk,qhd->kd/dot_general | solution.py:112
  288.7 3.7 all-to-all-start.1
  294.0 24.9 %all-to-all-done.1 = bf16[8,512,256]{1,2,0:T(8,128)(2,1)S(1)} async-done(((bf16[8,512,256]{1,2,0:T(8,128)(2,1)}), bf16[8,512,256]{1,2,0:T(8,128)(2,1)S(1)}, u32[]{:S(2)}, u32[]{:S(2)}) %all-to-all-start.1) | async-done | bytes 2097184 | tf_op jit(solution)/shard_map/all_to_all | solution.py:54
  322.3 4.5 %add_convert_fusion = bf16[512,4096]{1,0:T(8,128)(2,1)} fusion(f32[512,4096]{1,0:T(8,128)S(1)} %fusion.48, bf16[512,128]{0,1:T(8,128)(2,1)S(1)} %add_convert_fusion.1, bf16[4096,384]{1,0:T(8,128)(2,1)} %all-gather.3.cloned.1.call-done), kind=kOutput, calls=%fused_computation.47 | convolution fusion | flops 541065216 | bytes 13762560 | tf_op jit(solution)/shard_map/dot_general | solution.py:200
  327.0 4.0 convolution_convert_fusion
  331.3 52.4 %all_to_all.15 = bf16[8,512,384]{1,2,0:T(8,128)(2,1)S(1)} all-to-all(bf16[8,512,384]{1,2,0:T(8,128)(2,1)S(1)} %bitcast.184), channel_id=1, replica_groups=mesh['ctx'=8,'tp'=16] {'ctx'}, dimensions={0} | all-to-all | bytes 6291456 | tf_op jit(solution)/shard_map/all_to_all | solution.py:54
  386.0 27.9 %reduce-scatter.2.cloned.1.call-done = bf16[32,4096]{1,0:T(8,128)(2,1)} async-done(((bf16[512,4096]{1,0:T(8,128)(2,1)}), bf16[32,4096]{1,0:T(8,128)(2,1)}) %reduce-scatter.2.cloned.1.call-update) | async-done | bytes 262160 | tf_op jit(solution)/shard_map/reduce_scatter | solution.py:203
  (136 shorter events, 88.0 us)
Async XLA Ops:
  7.2 3.4 copy-start
  7.2 77.0 %all-gather.3.cloned.1.call-start = ((), (), s32[]{:S(2)}) async-start(), calls=%async_computation.4 | async-start | bytes 3538944 | tf_op jit(solution)/shard_map/all_gather | solution.py:13
  9.1 132.1 %all-gather.5.cloned.1.call-start = ((), (), s32[]{:S(2)}) async-start(), calls=%async_computation.5 | async-start | bytes 4456448 | tf_op jit(solution)/shard_map/all_gather | solution.py:136
  10.5 23.1 %copy-start.13 = (s32[4096]{0:T(1024)S(1)}, s32[4096]{0:T(1024)}, u32[]{:S(2)}) copy-start(s32[4096]{0:T(1024)} %param.12) | copy-start | bytes 49156
  145.2 4.1 collective-permute-start
  152.2 4.5 %copy-start.14 = (bf16[512,256]{1,0:T(8,128)(2,1)S(1)}, bf16[512,256]{1,0:T(8,128)(2,1)}, u32[]{:S(2)}) copy-start(bf16[512,256]{1,0:T(8,128)(2,1)} %param.9) | copy-start | bytes 786436
  152.2 31.8 %all-to-all-start = ((bf16[8,512,256]{1,2,0:T(8,128)(2,1)}), bf16[8,512,256]{1,2,0:T(8,128)(2,1)S(1)}, u32[]{:S(2)}, u32[]{:S(2)}) async-start(bf16[8,512,256]{1,2,0:T(8,128)(2,1)} %broadcast_in_dim.33), calls=%async_computation | async-start | bytes 4194304 | tf_op jit(solution)/shard_map/all_to_all | solution.py:32
  163.5 3.9 copy-start.12
  166.5 19.9 %copy-start.9 = (f32[512,128]{1,0:T(8,128)}, f32[512,128]{1,0:T(8,128)S(1)}, u32[]{:S(2)}) copy-start(f32[512,128]{1,0:T(8,128)S(1)} %copy.70) | copy-start | bytes 786436
  195.1 4.5 %copy-start.3 = (f32[2,128,4096]{2,1,0:T(8,128)S(1)}, f32[2,128,4096]{2,1,0:T(8,128)}, u32[]{:S(2)}) copy-start(f32[2,128,4096]{2,1,0:T(8,128)} %get-tuple-element.291) | copy-start | bytes 12582916 | tf_op jit(solution)/shard_map/while
  201.6 4.0 copy-start.2
  215.7 4.5 %copy-start.3 = (f32[2,128,4096]{2,1,0:T(8,128)S(1)}, f32[2,128,4096]{2,1,0:T(8,128)}, u32[]{:S(2)}) copy-start(f32[2,128,4096]{2,1,0:T(8,128)} %get-tuple-element.291) | copy-start | bytes 12582916 | tf_op jit(solution)/shard_map/while
  222.3 4.6 %copy-start.2 = (bf16[2,128,4096]{2,1,0:T(8,128)(2,1)S(1)}, bf16[2,128,4096]{2,1,0:T(8,128)(2,1)}, u32[]{:S(2)}) copy-start(bf16[2,128,4096]{2,1,0:T(8,128)(2,1)} %fusion.121) | copy-start | bytes 6291460 | tf_op jit(solution)/shard_map/while
  238.6 4.5 %copy-start.3 = (f32[2,128,4096]{2,1,0:T(8,128)S(1)}, f32[2,128,4096]{2,1,0:T(8,128)}, u32[]{:S(2)}) copy-start(f32[2,128,4096]{2,1,0:T(8,128)} %get-tuple-element.291) | copy-start | bytes 12582916 | tf_op jit(solution)/shard_map/while
  245.2 4.6 %copy-start.2 = (bf16[2,128,4096]{2,1,0:T(8,128)(2,1)S(1)}, bf16[2,128,4096]{2,1,0:T(8,128)(2,1)}, u32[]{:S(2)}) copy-start(bf16[2,128,4096]{2,1,0:T(8,128)(2,1)} %fusion.121) | copy-start | bytes 6291460 | tf_op jit(solution)/shard_map/while
  261.5 4.5 %copy-start.3 = (f32[2,128,4096]{2,1,0:T(8,128)S(1)}, f32[2,128,4096]{2,1,0:T(8,128)}, u32[]{:S(2)}) copy-start(f32[2,128,4096]{2,1,0:T(8,128)} %get-tuple-element.291) | copy-start | bytes 12582916 | tf_op jit(solution)/shard_map/while
  268.1 4.6 %copy-start.2 = (bf16[2,128,4096]{2,1,0:T(8,128)(2,1)S(1)}, bf16[2,128,4096]{2,1,0:T(8,128)(2,1)}, u32[]{:S(2)}) copy-start(bf16[2,128,4096]{2,1,0:T(8,128)(2,1)} %fusion.121) | copy-start | bytes 6291460 | tf_op jit(solution)/shard_map/while
  279.0 2.0 copy-start.5
  284.2 1.9 copy-start.8
  288.7 4.0 copy-start.11
  288.7 30.2 %all-to-all-start.1 = ((bf16[8,512,256]{1,2,0:T(8,128)(2,1)}), bf16[8,512,256]{1,2,0:T(8,128)(2,1)S(1)}, u32[]{:S(2)}, u32[]{:S(2)}) async-start(bf16[8,512,256]{1,2,0:T(8,128)(2,1)} %copy.84), calls=%async_computation.1 | async-start | bytes 4194304 | tf_op jit(solution)/shard_map/all_to_all | solution.py:54
  292.4 121.5 %reduce-scatter.2.cloned.1.call-start = ((), (), s32[]{:S(2)}) async-start(), calls=%async_computation.6 | async-start | bytes 4456448 | tf_op jit(solution)/shard_map/reduce_scatter | solution.py:203
  319.2 3.0 collective-permute-start.1
  383.6 30.3 %copy-start.1 = (s32[4096]{0:T(1024)S(1)}, s32[4096]{0:T(1024)}, u32[]{:S(2)}) copy-start(s32[4096]{0:T(1024)} %param.13) | copy-start | bytes 49156
  (4 other events, 4.9 us)
Sparse Core Ops, SparseCore 0:
  10.2 73.9 all-gather.2
  86.7 54.4 all-gather.4
  327.0 86.9 reduce-scatter.1
where the time goes:
time: 422 us; the launch traced here: 420 us
  waiting for transfers between devices  174 us (41%)
  matrix products  92 us (22%)
  blocking collectives  52.4 us (12%)
  local copies, waits for them, and re-layouts  52.2 us (12%)
  other arithmetic  26.7 us (6%)
  between operations  14.2 us (3%)
  starting transfers between devices  8.92 us (2%)
    all_gather x1, waiting for transfers between devices, shards(): gathered = lax.all_gather(tokens, 'tp', axis=0, tiled=True)  57 us
    all_to_all x1, blocking collectives, summed_on_arrival(): blocks = lax.all_to_all(cut_along(x, dim, count), axis, 0, 0, tiled=True)  52.4 us
    all_gather x1, waiting for transfers between devices, side_by_side(): lax.all_gather(both, axis, axis=dim, tiled=True)  50.6 us
    reduce_scatter x1, waiting for transfers between devices, shards(): lax.psum_scatter((part_query + part_keyval).astype(jnp.bfloat16), 'tp', s...  27.9 us
    all_to_all x1, waiting for transfers between devices, summed_on_arrival(): blocks = lax.all_to_all(cut_along(x, dim, count), axis, 0, 0, tiled=True)  24.9 us
    gather x1, local copies, waits for them, and re-layouts, shards(): doc_all = jnp.take(documents, positions)  23 us
    sub x4, matrix products, advance(): exponent = jnp.exp(scores - row_peak)  19.7 us
    dot_general x4, matrix products, advance(): jnp.einsum('hqk,qhd->kd', score_grad, query_block, preferred_element_type...  17.7 us
  transfers between devices with their start and end apart: 7, of which 5 were waited for; matrix products, arithmetic and copies ran while one was open for 13% of the time, Pallas kernels for 0%

commit v1 on v0

--- a/solution.py
+++ b/solution.py
@@ -133,7 +133,10 @@
     ctx_rank = lax.axis_index("ctx")
     tp_rank = lax.axis_index("tp")
     tensor_split_count = lax.axis_size("tp")
-    gathered = lax.all_gather(tokens, "tp", axis=0, tiled=True)
+    size = lax.axis_size("tp")
+    pieces = jnp.stack([tokens for _ in range(size)])
+    pieces = lax.all_to_all(pieces, "tp", split_axis=0, concat_axis=0)
+    gathered = jnp.concatenate(pieces, axis=0)
     tok_rows = gathered.shape[0]
     query_cols = w_query.shape[1]
     head_count = query_cols // HEAD_DIMENSION

time: 422 us -> 411 us (0.974)
  waiting for transfers between devices: 174 us -> 155 us
  starting transfers between devices: 8.92 us -> 16.4 us
    all_to_all x0 -> x1, waiting for transfers between devices: none -> 73.7 us  [shards(): pieces = lax.all_to_all(pieces, 'tp', split_axis=0, concat_axis=0)]
    all_gather x1 -> x0, waiting for transfers between devices: 57 us -> none  [shards(): gathered = lax.all_gather(tokens, 'tp', axis=0, tiled=True)]
    all_gather x1, waiting for transfers between devices: 50.6 us -> 11.2 us  [side_by_side(): lax.all_gather(both, axis, axis=dim, tiled=True)]
    all_to_all x0 -> x1, starting transfers between devices: none -> 8.17 us  [shards(): pieces = lax.all_to_all(pieces, 'tp', split_axis=0, concat_axis=0)]
    reduce_scatter x1, waiting for transfers between devices: 27.9 us -> 32.2 us  [shards(): lax.psum_scatter((part_query + part_keyval).astype(jnp.bfloat16), 'tp', s...]
  transfers between devices with their start and end apart: 7 -> 7, of which waited for: 5 -> 5; matrix products, arithmetic and copies ran while one was open for 13% -> 14% of each run, Pallas kernels for 0% -> 0%
where the time goes in v1:
time: 411 us; the launch traced here: 409 us
  waiting for transfers between devices  155 us (38%)
  matrix products  91.9 us (22%)
  local copies, waits for them, and re-layouts  55.6 us (14%)
  blocking collectives  49.5 us (12%)
  other arithmetic  26 us (6%)
  starting transfers between devices  16.4 us (4%)
  between operations  14.5 us (4%)
    all_to_all x1, waiting for transfers between devices, shards(): pieces = lax.all_to_all(pieces, 'tp', split_axis=0, concat_axis=0)  73.7 us
    all_to_all x1, blocking collectives, summed_on_arrival(): blocks = lax.all_to_all(cut_along(x, dim, count), axis, 0, 0, tiled=True)  49.5 us
    reduce_scatter x1, waiting for transfers between devices, shards(): lax.psum_scatter((part_query + part_keyval).astype(jnp.bfloat16), 'tp', s...  32.2 us
    all_to_all x1, waiting for transfers between devices, summed_on_arrival(): blocks = lax.all_to_all(cut_along(x, dim, count), axis, 0, 0, tiled=True)  25.1 us
    gather x1, local copies, waits for them, and re-layouts, shards(): doc_all = jnp.take(documents, positions)  23 us
    sub x4, matrix products, advance(): exponent = jnp.exp(scores - row_peak)  19.6 us
    dot_general x4, matrix products, advance(): jnp.einsum('hqk,qhd->kd', score_grad, query_block, preferred_element_type...  17.8 us
    all_to_all x1, waiting for transfers between devices, copy_for_each(): lax.all_to_all(jnp.broadcast_to(x[None], (count, *x.shape)), axis, 0, 0,...  13.1 us
  transfers between devices with their start and end apart: 7, of which 5 were waited for; matrix products, arithmetic and copies ran while one was open for 14% of the time, Pallas kernels for 0%

profile of v1, /device:TPU:0, one launch (start us, length us, event | category | flops | bytes accessed | tf_op | source)
XLA Modules:
  0.0 409.4 jit_solution(15835393459151553913)
XLA Ops:
  12.5 8.2 %all-to-all-start = ((bf16[16,32,4096]{2,1,0:T(8,128)(2,1)}), bf16[16,32,4096]{2,1,0:T(8,128)(2,1)}, u32[]{:S(2)}, u32[]{:S(2)}) async-start(bf16[16,32,4096]{2,1,0:T(8,128)(2,1)} %stack.2), calls=%async_computation | async-start | bytes 8388608 | tf_op jit(solution)/shard_map/all_to_all | solution.py:138
  20.7 23.0 %gather_fusion = s32[4096]{0:T(1024)S(1)} fusion(s32[4096]{0:T(1024)S(1)} %copy-done, s32[4096]{0:T(1024)S(1)} %fusion.68), kind=kCustom, calls=%fused_computation | custom fusion | bytes 49152 | tf_op jit(solution)/shard_map/jit(_take)/gather | solution.py:144
  43.8 73.7 %all-to-all-done = bf16[16,32,4096]{2,1,0:T(8,128)(2,1)} async-done(((bf16[16,32,4096]{2,1,0:T(8,128)(2,1)}), bf16[16,32,4096]{2,1,0:T(8,128)(2,1)}, u32[]{:S(2)}, u32[]{:S(2)}) %all-to-all-start) | async-done | bytes 4194336 | tf_op jit(solution)/shard_map/all_to_all | solution.py:138
  117.5 11.2 %all-gather.2.cloned.1.call-done = bf16[4096,384]{1,0:T(8,128)(2,1)} async-done(((bf16[512,384]{1,0:T(8,128)(2,1)}), bf16[4096,384]{1,0:T(8,128)(2,1)}) %all-gather.2.cloned.1.call-update) | async-done | bytes 3145744 | tf_op jit(solution)/shard_map/all_gather | solution.py:13
  128.7 4.0 fusion.52
  132.8 3.7 multiply_cosine_fusion
  139.5 4.0 all-to-all-start.1
  144.4 4.1 %fusion.50 = f32[256,512]{1,0:T(8,128)S(1)} fusion(bf16[512,4096]{1,0:T(8,128)(2,1)} %bitcast.2, bf16[4096,384]{1,0:T(8,128)(2,1)} %all-gather.2.cloned.1.call-done), kind=kOutput, calls=%fused_computation.66 | convolution fusion | flops 1073741824 | bytes 6815744 | tf_op jit(solution)/shard_map/dot_general | solution.py:152
  158.1 13.1 %all-to-all-done.1 = bf16[8,512,256]{1,2,0:T(8,128)(2,1)S(1)} async-done(((bf16[8,512,256]{1,2,0:T(8,128)(2,1)}), bf16[8,512,256]{1,2,0:T(8,128)(2,1)S(1)}, u32[]{:S(2)}, u32[]{:S(2)}) %all-to-all-start.1) | async-done | bytes 2097184 | tf_op jit(solution)/shard_map/all_to_all | solution.py:32
  176.7 89.3 %while.15 = (s32[]{:T(128)}, f32[4096,128]{1,0:T(8,128)}, f32[4096,128]{1,0:T(8,128)}, f32[4,128,2,128]{3,1,2,0:T(8,128)}, s32[4096]{0:T(1024)S(1)}, /*index=5*/...) while((s32[]{:T(128)}, f32[4096,128]{1,0:T(8,128)}, ...), condition=%wide.region_4.5_spmd.clone, body=%wide.region_0.4_spmd.clone.sunk | while | flops 1625427712 | bytes 64595660 | solution.py:127
  177.2 4.9 %fusion.118 = (f32[2,128]{1,0:T(2,128)S(1)}, f32[2,128,4096]{2,1,0:T(8,128)}) fusion(pred[128,4096]{1,0:T(8,128)(4,1)S(1)} %compare_and_fusion.2, bf16[4096,128]{1,0:T(8,128)(2,1)} %get-tuple-element.330, bf16[4,128,2,128]{3,1,2,0:T(8,128)(2,1)} %get-tuple-element.329, s32[]{:T(128)} %get-tuple-element.307), kind=kOutput, calls=%fused_computation.112.clone.1 | convolution fusion | flops 272633856 | bytes 5834240 | tf_op jit(solution)/shard_map/while/body/eval_jaxpr/sub | solution.py:100
  188.7 4.0 fusion.122
  197.9 4.9 %fusion.118 = (f32[2,128]{1,0:T(2,128)S(1)}, f32[2,128,4096]{2,1,0:T(8,128)}) fusion(pred[128,4096]{1,0:T(8,128)(4,1)S(1)} %compare_and_fusion.2, bf16[4096,128]{1,0:T(8,128)(2,1)} %get-tuple-element.330, bf16[4,128,2,128]{3,1,2,0:T(8,128)(2,1)} %get-tuple-element.329, s32[]{:T(128)} %get-tuple-element.307), kind=kOutput, calls=%fused_computation.112.clone.1 | convolution fusion | flops 272633856 | bytes 5834240 | tf_op jit(solution)/shard_map/while/body/eval_jaxpr/sub | solution.py:100
  209.4 4.6 %fusion.122 = f32[4096,128]{1,0:T(8,128)} fusion(bf16[2,128,4096]{2,1,0:T(8,128)(2,1)} %fusion.121, f32[4096,128]{1,0:T(8,128)} %get-tuple-element.308, pred[]{:T(512)S(6)} %compare.5, bf16[4,128,2,128]{3,1,2,0:T(8,128)(2,1)} %get-tuple-element.329, s32[]{:T(128)} %get-tuple-element.307), kind=kOutput, calls=%fused_computation.14.clone.1 | convolution fusion | flops 270008320 | bytes 6357505 | tf_op jit(solution)/shard_map/while/body/eval_jaxpr/hqk,qhd->kd/dot_general | solution.py:112
  220.7 4.9 %fusion.118 = (f32[2,128]{1,0:T(2,128)S(1)}, f32[2,128,4096]{2,1,0:T(8,128)}) fusion(pred[128,4096]{1,0:T(8,128)(4,1)S(1)} %compare_and_fusion.2, bf16[4096,128]{1,0:T(8,128)(2,1)} %get-tuple-element.330, bf16[4,128,2,128]{3,1,2,0:T(8,128)(2,1)} %get-tuple-element.329, s32[]{:T(128)} %get-tuple-element.307), kind=kOutput, calls=%fused_computation.112.clone.1 | convolution fusion | flops 272633856 | bytes 5834240 | tf_op jit(solution)/shard_map/while/body/eval_jaxpr/sub | solution.py:100
  232.2 4.6 %fusion.122 = f32[4096,128]{1,0:T(8,128)} fusion(bf16[2,128,4096]{2,1,0:T(8,128)(2,1)} %fusion.121, f32[4096,128]{1,0:T(8,128)} %get-tuple-element.308, pred[]{:T(512)S(6)} %compare.5, bf16[4,128,2,128]{3,1,2,0:T(8,128)(2,1)} %get-tuple-element.329, s32[]{:T(128)} %get-tuple-element.307), kind=kOutput, calls=%fused_computation.14.clone.1 | convolution fusion | flops 270008320 | bytes 6357505 | tf_op jit(solution)/shard_map/while/body/eval_jaxpr/hqk,qhd->kd/dot_general | solution.py:112
  243.6 4.9 %fusion.118 = (f32[2,128]{1,0:T(2,128)S(1)}, f32[2,128,4096]{2,1,0:T(8,128)}) fusion(pred[128,4096]{1,0:T(8,128)(4,1)S(1)} %compare_and_fusion.2, bf16[4096,128]{1,0:T(8,128)(2,1)} %get-tuple-element.330, bf16[4,128,2,128]{3,1,2,0:T(8,128)(2,1)} %get-tuple-element.329, s32[]{:T(128)} %get-tuple-element.307), kind=kOutput, calls=%fused_computation.112.clone.1 | convolution fusion | flops 272633856 | bytes 5834240 | tf_op jit(solution)/shard_map/while/body/eval_jaxpr/sub | solution.py:100
  255.1 4.6 %fusion.122 = f32[4096,128]{1,0:T(8,128)} fusion(bf16[2,128,4096]{2,1,0:T(8,128)(2,1)} %fusion.121, f32[4096,128]{1,0:T(8,128)} %get-tuple-element.308, pred[]{:T(512)S(6)} %compare.5, bf16[4,128,2,128]{3,1,2,0:T(8,128)(2,1)} %get-tuple-element.329, s32[]{:T(128)} %get-tuple-element.307), kind=kOutput, calls=%fused_computation.14.clone.1 | convolution fusion | flops 270008320 | bytes 6357505 | tf_op jit(solution)/shard_map/while/body/eval_jaxpr/hqk,qhd->kd/dot_general | solution.py:112
  275.7 3.7 all-to-all-start.2
  281.0 25.1 %all-to-all-done.2 = bf16[8,512,256]{1,2,0:T(8,128)(2,1)S(1)} async-done(((bf16[8,512,256]{1,2,0:T(8,128)(2,1)}), bf16[8,512,256]{1,2,0:T(8,128)(2,1)S(1)}, u32[]{:S(2)}, u32[]{:S(2)}) %all-to-all-start.2) | async-done | bytes 2097184 | tf_op jit(solution)/shard_map/all_to_all | solution.py:54
  309.5 4.5 %add_convert_fusion = bf16[512,4096]{1,0:T(8,128)(2,1)} fusion(f32[512,4096]{1,0:T(8,128)S(1)} %fusion.48, bf16[512,128]{0,1:T(8,128)(2,1)S(1)} %add_convert_fusion.1, bf16[4096,384]{1,0:T(8,128)(2,1)} %all-gather.2.cloned.1.call-done), kind=kOutput, calls=%fused_computation.47 | convolution fusion | flops 541065216 | bytes 13762560 | tf_op jit(solution)/shard_map/dot_general | solution.py:203
  314.2 4.0 convolution_convert_fusion
  318.5 49.5 %all_to_all.20 = bf16[8,512,384]{1,2,0:T(8,128)(2,1)S(1)} all-to-all(bf16[8,512,384]{1,2,0:T(8,128)(2,1)S(1)} %bitcast.185), channel_id=1, replica_groups=mesh['ctx'=8,'tp'=16] {'ctx'}, dimensions={0} | all-to-all | bytes 6291456 | tf_op jit(solution)/shard_map/all_to_all | solution.py:54
  370.4 32.2 %reduce-scatter.2.cloned.1.call-done = bf16[32,4096]{1,0:T(8,128)(2,1)} async-done(((bf16[512,4096]{1,0:T(8,128)(2,1)}), bf16[32,4096]{1,0:T(8,128)(2,1)}) %reduce-scatter.2.cloned.1.call-update) | async-done | bytes 262160 | tf_op jit(solution)/shard_map/reduce_scatter | solution.py:206
  (136 shorter events, 93.3 us)
Async XLA Ops:
  7.2 13.6 %copy-start = (s32[4096]{0:T(1024)S(1)}, s32[4096]{0:T(1024)}, u32[]{:S(2)}) copy-start(s32[4096]{0:T(1024)} %param.13) | copy-start | bytes 49156
  7.2 121.5 %all-gather.2.cloned.1.call-start = ((), (), s32[]{:S(2)}) async-start(), calls=%async_computation.5 | async-start | bytes 3538944 | tf_op jit(solution)/shard_map/all_gather | solution.py:13
  12.5 8.2 %copy-start.13 = (s32[4096]{0:T(1024)S(1)}, s32[4096]{0:T(1024)}, u32[]{:S(2)}) copy-start(s32[4096]{0:T(1024)} %param.12) | copy-start | bytes 49156
  12.5 105.0 %all-to-all-start = ((bf16[16,32,4096]{2,1,0:T(8,128)(2,1)}), bf16[16,32,4096]{2,1,0:T(8,128)(2,1)}, u32[]{:S(2)}, u32[]{:S(2)}) async-start(bf16[16,32,4096]{2,1,0:T(8,128)(2,1)} %stack.2), calls=%async_computation | async-start | bytes 8388608 | tf_op jit(solution)/shard_map/all_to_all | solution.py:138
  132.7 3.8 collective-permute-start
  139.5 4.0 copy-start.14
  139.5 31.7 %all-to-all-start.1 = ((bf16[8,512,256]{1,2,0:T(8,128)(2,1)}), bf16[8,512,256]{1,2,0:T(8,128)(2,1)S(1)}, u32[]{:S(2)}, u32[]{:S(2)}) async-start(bf16[8,512,256]{1,2,0:T(8,128)(2,1)} %broadcast_in_dim.33), calls=%async_computation.1 | async-start | bytes 4194304 | tf_op jit(solution)/shard_map/all_to_all | solution.py:32
  150.3 3.9 copy-start.12
  153.4 20.2 %copy-start.9 = (f32[512,128]{1,0:T(8,128)}, f32[512,128]{1,0:T(8,128)S(1)}, u32[]{:S(2)}) copy-start(f32[512,128]{1,0:T(8,128)S(1)} %copy.70) | copy-start | bytes 786436
  182.1 4.5 %copy-start.3 = (f32[2,128,4096]{2,1,0:T(8,128)S(1)}, f32[2,128,4096]{2,1,0:T(8,128)}, u32[]{:S(2)}) copy-start(f32[2,128,4096]{2,1,0:T(8,128)} %get-tuple-element.291) | copy-start | bytes 12582916 | tf_op jit(solution)/shard_map/while
  188.7 4.0 copy-start.2
  202.8 4.5 %copy-start.3 = (f32[2,128,4096]{2,1,0:T(8,128)S(1)}, f32[2,128,4096]{2,1,0:T(8,128)}, u32[]{:S(2)}) copy-start(f32[2,128,4096]{2,1,0:T(8,128)} %get-tuple-element.291) | copy-start | bytes 12582916 | tf_op jit(solution)/shard_map/while
  209.3 4.6 %copy-start.2 = (bf16[2,128,4096]{2,1,0:T(8,128)(2,1)S(1)}, bf16[2,128,4096]{2,1,0:T(8,128)(2,1)}, u32[]{:S(2)}) copy-start(bf16[2,128,4096]{2,1,0:T(8,128)(2,1)} %fusion.121) | copy-start | bytes 6291460 | tf_op jit(solution)/shard_map/while
  225.6 4.5 %copy-start.3 = (f32[2,128,4096]{2,1,0:T(8,128)S(1)}, f32[2,128,4096]{2,1,0:T(8,128)}, u32[]{:S(2)}) copy-start(f32[2,128,4096]{2,1,0:T(8,128)} %get-tuple-element.291) | copy-start | bytes 12582916 | tf_op jit(solution)/shard_map/while
  232.2 4.6 %copy-start.2 = (bf16[2,128,4096]{2,1,0:T(8,128)(2,1)S(1)}, bf16[2,128,4096]{2,1,0:T(8,128)(2,1)}, u32[]{:S(2)}) copy-start(bf16[2,128,4096]{2,1,0:T(8,128)(2,1)} %fusion.121) | copy-start | bytes 6291460 | tf_op jit(solution)/shard_map/while
  248.5 4.5 %copy-start.3 = (f32[2,128,4096]{2,1,0:T(8,128)S(1)}, f32[2,128,4096]{2,1,0:T(8,128)}, u32[]{:S(2)}) copy-start(f32[2,128,4096]{2,1,0:T(8,128)} %get-tuple-element.291) | copy-start | bytes 12582916 | tf_op jit(solution)/shard_map/while
  255.1 4.6 %copy-start.2 = (bf16[2,128,4096]{2,1,0:T(8,128)(2,1)S(1)}, bf16[2,128,4096]{2,1,0:T(8,128)(2,1)}, u32[]{:S(2)}) copy-start(bf16[2,128,4096]{2,1,0:T(8,128)(2,1)} %fusion.121) | copy-start | bytes 6291460 | tf_op jit(solution)/shard_map/while
  266.0 2.0 copy-start.5
  271.1 1.9 copy-start.8
  275.7 4.0 copy-start.11
  275.7 30.5 %all-to-all-start.2 = ((bf16[8,512,256]{1,2,0:T(8,128)(2,1)}), bf16[8,512,256]{1,2,0:T(8,128)(2,1)S(1)}, u32[]{:S(2)}, u32[]{:S(2)}) async-start(bf16[8,512,256]{1,2,0:T(8,128)(2,1)} %copy.84), calls=%async_computation.2 | async-start | bytes 4194304 | tf_op jit(solution)/shard_map/all_to_all | solution.py:54
  279.4 123.2 %reduce-scatter.2.cloned.1.call-start = ((), (), s32[]{:S(2)}) async-start(), calls=%async_computation.6 | async-start | bytes 4456448 | tf_op jit(solution)/shard_map/reduce_scatter | solution.py:206
  306.5 3.0 collective-permute-start.1
  368.0 34.6 %copy-start.1 = (s32[4096]{0:T(1024)S(1)}, s32[4096]{0:T(1024)}, u32[]{:S(2)}) copy-start(s32[4096]{0:T(1024)} %param.13) | copy-start | bytes 49156
  (4 other events, 5.0 us)
Sparse Core Ops, SparseCore 0:
  10.2 118.4 all-gather.1
  314.2 88.3 reduce-scatter.1
